TPU v7x, 512 devices: a whole 4x8x8 slice. The times are simulated.
512 devices in a mesh: band: 64 (over y, z), lev: 8 (over x, core).
Axes of the slice: x: 4, y: 8, z: 8, core: 2. Of those that a mesh axis runs over, the one named last changes fastest.
Arguments:
- concentration: float32 [4, 8, 128, 256], P(None, 'lev', 'band'), may hold values from 0.1 to 2
- target: float32 [4, 8, 128, 256], P(None, 'lev', 'band'), may hold values from -6 to 6
- zonal_wind: float32 [8, 128, 256], P('lev', 'band'), may hold values from -0.6 to 0.6
- merid_wind: float32 [8, 128, 256], P('lev', 'band'), may hold values from -0.6 to 0.6
- sea_mask: int32 [128, 256], P('band'), may hold values 0 or 1
- first_weight: float32 [2, 20, 128], replicated, may hold values from -1.25 to 1.25
- first_bias: float32 [2, 128], replicated, may hold values from -3 to 3
- middle_weight: float32 [2, 128, 128], replicated, may hold values from -0.5 to 0.5
- middle_bias: float32 [2, 128], replicated, may hold values from -3 to 3
- last_weight: float32 [2, 4, 128], replicated, may hold values from -0.125 to 0.125
- last_bias: float32 [2, 4], replicated, may hold values from -0.6 to 0.6
Outputs:
- final_field: float32 [4, 8, 128, 256], P(None, 'lev', 'band')
- first_weight_grad: float32 [2, 20, 128], replicated
- first_bias_grad: float32 [2, 128], replicated
- middle_weight_grad: float32 [2, 128, 128], replicated
- middle_bias_grad: float32 [2, 128], replicated
- last_weight_grad: float32 [2, 4, 128], replicated
- last_bias_grad: float32 [2, 4], replicated
Inputs may be any that keep to these rules, and one draw needn't show every extreme that they name: `sea_mask`: 1 marks a sea cell, 0 a land cell.
All inputs are finite; a program needn't handle non-finite values. No bound on the sum of `sea_mask` on one device may be relied on, other than what follows from the above.
Results may differ from a plain program's by a relative error of at most 0.00013.
Values sent between devices are 32-bit elements; how exact they have to be, the bound alone decides.
A program may use at most 64 MiB of HBM per device.

v0:
```python
import math
import jax
import jax.numpy as jnp
from jax import lax
from jax.sharding import PartitionSpec as P

STEPS = 3
stencil_base = (-1.0 / 12.0, 7.0 / 12.0, 7.0 / 12.0, -1.0 / 12.0)


def cut_along(array, direction, start, length):
    return lax.slice_in_dim(array, start, start + length, axis=direction)


def pad_along(array, direction, width):
    widths = [(0, 0)] * array.ndim
    widths[direction] = (width, width)
    return jnp.pad(array, widths)


def face_flux(network, stencil, courant, mask_low, mask_high):
    w_first, b_first, w_second, b_second, w_last, b_last = network
    face_shape = courant.shape
    columns = courant.size
    nbins = stencil.shape[1]
    features = jnp.concatenate(
        [
            stencil.reshape(4 * nbins, columns),
            courant.reshape(1, columns),
            (courant * courant).reshape(1, columns),
            mask_low.reshape(1, columns),
            mask_high.reshape(1, columns),
        ],
        0,
    )
    hidden_one = jnp.tanh(
        jnp.dot(w_first.T, features, precision=lax.Precision.HIGHEST) + b_first[:, None]
    )
    hidden_two = jnp.tanh(
        jnp.dot(w_second.T, hidden_one, precision=lax.Precision.HIGHEST) + b_second[:, None]
    )
    output = jnp.dot(w_last, hidden_two, precision=lax.Precision.HIGHEST) + b_last[:, None]
    correction = output - jnp.mean(output, 0, keepdims=True)
    weights_face = jnp.asarray(stencil_base, jnp.float32)[:, None] + correction
    face_value = jnp.sum(weights_face.reshape((4, 1) + face_shape) * stencil, 0)
    return courant[None] * face_value


def advance(network, padded, wind_padded, mask_padded, direction):
    length = padded.shape[direction] - 4
    stencil = jnp.stack([cut_along(padded, direction, offset, length + 1) for offset in range(4)])
    courant = 0.5 * (
        cut_along(wind_padded, direction - 1, 0, length + 1)
        + cut_along(wind_padded, direction - 1, 1, length + 1)
    )
    mask_low = cut_along(mask_padded, direction - 1, 0, length + 1)
    mask_high = cut_along(mask_padded, direction - 1, 1, length + 1)
    fluxes = face_flux(network, stencil, courant, mask_low, mask_high)
    centre = cut_along(padded, direction, 2, length)
    return centre - (
        cut_along(fluxes, direction, 1, length) - cut_along(fluxes, direction, 0, length)
    )


def to_columns(field):
    return lax.all_to_all(field, "band", split_axis=3, concat_axis=2, tiled=True)


def to_rows(field):
    return lax.all_to_all(field, "band", split_axis=2, concat_axis=3, tiled=True)


def on_device(
    concentration,
    target,
    zonal_wind,
    merid_wind,
    sea_mask,
    first_weight,
    first_bias,
    middle_weight,
    middle_bias,
    last_weight,
    last_bias,
):
    params = (first_weight, first_bias, middle_weight, middle_bias, last_weight, last_bias)
    zonal_net = tuple((member[0] for member in params))
    merid_net = tuple((member[1] for member in params))
    bins_here, levels_here, row_count, col_count = concentration.shape
    total_cells = (
        bins_here
        * levels_here
        * row_count
        * col_count
        * lax.axis_size("band")
        * lax.axis_size("lev")
    )
    loss_scale = 1.0 / math.sqrt(total_cells)
    sea_field = sea_mask.astype(jnp.float32)[None]
    wind_zonal = pad_along(zonal_wind, 2, 1)
    mask_zonal = pad_along(sea_field, 2, 1)
    stacked = jnp.concatenate([merid_wind, sea_field], 0)
    columns_data = lax.all_to_all(stacked, "band", split_axis=2, concat_axis=1, tiled=True)
    wind_merid = pad_along(columns_data[:levels_here], 1, 1)
    mask_merid = pad_along(columns_data[levels_here:], 1, 1)

    def zonal_sweep(network, padded):
        return advance(network, padded, wind_zonal, mask_zonal, 3)

    def merid_sweep(network, padded):
        return advance(network, padded, wind_merid, mask_merid, 2)

    pullbacks = []
    field = concentration
    for step_number in range(STEPS):
        field, zonal_back = jax.vjp(zonal_sweep, zonal_net, pad_along(field, 3, 2))
        moved, merid_back = jax.vjp(merid_sweep, merid_net, pad_along(to_columns(field), 2, 2))
        field = to_rows(moved)
        pullbacks.append((zonal_back, merid_back))
    cotangent = (field - target) * loss_scale
    sums = tuple((jnp.zeros_like(member) for member in params))
    for step_number in reversed(range(STEPS)):
        zonal_back, merid_back = pullbacks[step_number]
        merid_grads, padded_grad = merid_back(to_columns(cotangent))
        cotangent = to_rows(padded_grad[:, :, 2:-2])
        zonal_grads, padded_grad = zonal_back(cotangent)
        cotangent = padded_grad[:, :, :, 2:-2]
        step_grads = tuple(
            (
                jnp.stack([zonal_part, merid_part])
                for zonal_part, merid_part in zip(zonal_grads, merid_grads)
            )
        )
        sums = tuple((earlier + latest for earlier, latest in zip(sums, step_grads)))
    sums = lax.psum((sums[0], sums[1], sums[2], sums[3], sums[4], sums[5]), ("band", "lev"))
    return (field, sums[0], sums[1], sums[2], sums[3], sums[4], sums[5])


def solution(mesh):
    return jax.shard_map(
        on_device,
        mesh=mesh,
        in_specs=(
            P(None, "lev", "band", None),
            P(None, "lev", "band", None),
            P("lev", "band", None),
            P("lev", "band", None),
            P("band", None),
            P(),
            P(),
            P(),
            P(),
            P(),
            P(),
        ),
        out_specs=(P(None, "lev", "band", None), P(), P(), P(), P(), P(), P()),
        check_vma=False,
    )
```

profile of v0, /device:TPU:1, one launch (start us, length us, event | category | flops | bytes accessed | tf_op | source)
XLA Modules:
  0.0 649.2 jit_solution(2578516520645093349)
XLA Ops:
  9.5 17.3 %all-to-all-start.1 = ((f32[2,2,256]{1,0,2:T(2,128)}), f32[2,2,256]{1,0,2:T(2,128)S(1)}, u32[]{:S(2)}, u32[]{:S(2)}) async-start(f32[2,2,256]{1,0,2:T(2,128)} %copy.634), calls=%async_computation.1 | async-start | bytes 524288 | tf_op jit(solution)/shard_map/all_to_all | solution.py:103
  36.5 3.0 all-to-all-done.1
  39.6 9.1 %all-to-all-start = ((f32[4,1,2,256]{0,2,1,3:T(2,128)}), f32[4,1,2,256]{0,2,1,3:T(2,128)S(1)}, u32[]{:S(2)}, u32[]{:S(2)}) async-start(f32[4,1,2,256]{0,2,1,3:T(2,128)} %copy.631), calls=%async_computation | async-start | bytes 524288 | tf_op jit(solution)/shard_map/all_to_all | solution.py:66
  50.4 10.8 %all-to-all-done = f32[4,1,2,256]{0,2,1,3:T(2,128)S(1)} async-done(((f32[4,1,2,256]{0,2,1,3:T(2,128)}), f32[4,1,2,256]{0,2,1,3:T(2,128)S(1)}, u32[]{:S(2)}, u32[]{:S(2)}) %all-to-all-start) | async-done | bytes 8224 | tf_op jit(solution)/shard_map/all_to_all | solution.py:66
  66.5 18.4 %all_to_all.231 = f32[4,1,128,4]{3,0,1,2:T(4,128)S(1)} all-to-all(f32[4,1,128,4]{3,0,1,2:T(4,128)S(1)} %copy.642), channel_id=1, replica_groups=mesh['band'=64,'lev'=8] {'band'}, dimensions={2} | all-to-all | bytes 16384 | tf_op jit(solution)/shard_map/all_to_all | solution.py:70
  88.9 18.4 %all_to_all.232 = f32[4,1,2,256]{0,2,1,3:T(2,128)S(1)} all-to-all(f32[4,1,2,256]{0,2,1,3:T(2,128)S(1)} %copy.646), channel_id=1, replica_groups=mesh['band'=64,'lev'=8] {'band'}, dimensions={3} | all-to-all | bytes 16384 | tf_op jit(solution)/shard_map/all_to_all | solution.py:66
  110.4 1.5 concatenate.121
  111.9 1.3 fusion.8
  113.3 1.2 fusion.2
  115.2 1.0 fusion.101
  117.3 18.4 %all_to_all.233 = f32[4,1,128,4]{3,0,1,2:T(4,128)S(1)} all-to-all(f32[4,1,128,4]{3,0,1,2:T(4,128)S(1)} %copy.651), channel_id=1, replica_groups=mesh['band'=64,'lev'=8] {'band'}, dimensions={2} | all-to-all | bytes 16384 | tf_op jit(solution)/shard_map/all_to_all | solution.py:70
  139.6 18.4 %all_to_all.234 = f32[4,1,2,256]{0,2,1,3:T(2,128)S(1)} all-to-all(f32[4,1,2,256]{0,2,1,3:T(2,128)S(1)} %copy.655), channel_id=1, replica_groups=mesh['band'=64,'lev'=8] {'band'}, dimensions={3} | all-to-all | bytes 16384 | tf_op jit(solution)/shard_map/all_to_all | solution.py:66
  160.7 1.5 slice_bitcast_fusion.15
  162.2 1.1 pad_maximum_fusion.2
  163.3 2.2 reshape.1580
  165.5 2.7 concatenate.123
  168.2 1.5 fusion.6
  169.7 1.2 fusion
  171.6 1.0 fusion.103
  172.7 1.3 add_bitcast_fusion
  174.0 1.6 mul.546
  175.5 1.9 multiply_reduce_fusion
  177.4 1.7 copy.716
  179.9 1.4 fusion.44
  181.2 1.6 copy.660
  182.8 18.8 %all_to_all.235 = f32[4,1,128,4]{3,0,1,2:T(4,128)S(1)} all-to-all(f32[4,1,128,4]{3,0,1,2:T(4,128)} %copy.660), channel_id=1, replica_groups=mesh['band'=64,'lev'=8] {'band'}, dimensions={2} | all-to-all | bytes 16384 | tf_op jit(solution)/shard_map/all_to_all | solution.py:70
  202.4 1.7 all_to_all.193
  204.1 1.3 fusion.50
  205.5 1.6 copy.664
  207.0 18.1 %all_to_all.236 = f32[4,1,2,256]{0,2,1,3:T(2,128)} all-to-all(f32[4,1,2,256]{0,2,1,3:T(2,128)} %copy.664), channel_id=1, replica_groups=mesh['band'=64,'lev'=8] {'band'}, dimensions={3} | all-to-all | bytes 16384 | tf_op jit(solution)/shard_map/all_to_all | solution.py:66
  225.2 2.6 copy.711
  227.8 1.9 copy.666
  229.7 1.7 copy.667
  232.0 1.4 multiply_bitcast_fusion.2
  233.4 1.6 copy.669
  235.0 1.9 multiply_reduce_fusion.7
  237.6 1.7 reshape.1587
  239.3 1.6 fusion.90
  241.1 1.2 fusion.110
  242.2 1.3 convolution_bitcast_fusion.4
  243.6 1.1 fusion.104
  246.6 1.1 reshape.1581
  247.7 1.1 bitcast_add_fusion.2
  250.9 4.7 all-to-all-start.8
  255.6 1.5 convolution_bitcast_fusion.21
  257.2 11.0 %all-to-all-done.8 = f32[4,1,128,4]{3,0,1,2:T(4,128)S(1)} async-done(((f32[4,1,128,4]{3,0,1,2:T(4,128)}), f32[4,1,128,4]{3,0,1,2:T(4,128)S(1)}, u32[]{:S(2)}, u32[]{:S(2)}) %all-to-all-start.8) | async-done | bytes 8224 | tf_op jit(solution)/shard_map/all_to_all | solution.py:70
  269.6 1.2 fusion.111
  270.8 1.3 convolution_bitcast_fusion.5
  272.1 1.1 fusion.105
  275.7 5.0 all-to-all-start.9
  281.5 11.8 %all-to-all-done.9 = f32[4,1,2,256]{0,2,1,3:T(2,128)S(1)} async-done(((f32[4,1,2,256]{0,2,1,3:T(2,128)}), f32[4,1,2,256]{0,2,1,3:T(2,128)S(1)}, u32[]{:S(2)}, u32[]{:S(2)}) %all-to-all-start.9) | async-done | bytes 8224 | tf_op jit(solution)/shard_map/all_to_all | solution.py:66
  293.3 1.0 copy.712
  298.0 1.2 fusion.112
  299.1 1.3 convolution_bitcast_fusion.2
  300.5 1.1 fusion.106
  305.4 4.7 all-to-all-start.10
  310.4 12.3 %all-to-all-done.10 = f32[4,1,128,4]{3,0,1,2:T(4,128)S(1)} async-done(((f32[4,1,128,4]{3,0,1,2:T(4,128)}), f32[4,1,128,4]{3,0,1,2:T(4,128)S(1)}, u32[]{:S(2)}, u32[]{:S(2)}) %all-to-all-start.10) | async-done | bytes 8224 | tf_op jit(solution)/shard_map/all_to_all | solution.py:70
  327.3 4.8 all-to-all-start.11
  332.3 12.3 %all-to-all-done.11 = f32[4,1,2,256]{0,2,1,3:T(2,128)S(1)} async-done(((f32[4,1,2,256]{0,2,1,3:T(2,128)}), f32[4,1,2,256]{0,2,1,3:T(2,128)S(1)}, u32[]{:S(2)}, u32[]{:S(2)}) %all-to-all-start.11) | async-done | bytes 8224 | tf_op jit(solution)/shard_map/all_to_all | solution.py:66
  351.7 4.7 all-to-all-start.12
  356.7 12.2 %all-to-all-done.12 = f32[4,1,128,4]{3,0,1,2:T(4,128)S(1)} async-done(((f32[4,1,128,4]{3,0,1,2:T(4,128)}), f32[4,1,128,4]{3,0,1,2:T(4,128)S(1)}, u32[]{:S(2)}, u32[]{:S(2)}) %all-to-all-start.12) | async-done | bytes 8224 | tf_op jit(solution)/shard_map/all_to_all | solution.py:70
  373.4 104.7 %all-reduce.47 = (f32[2,20,128]{2,1,0:T(8,128)S(1)}, f32[2,128]{1,0:T(2,128)}, f32[2,128]{1,0:T(2,128)}, f32[2,4,128]{2,1,0:T(4,128)}, f32[2,4]{1,0:T(2,128)}) all-reduce(f32[2,20,128]{2,1,0:T(8,128)S(1)} %fusion.37, f32[2,128]{1,0:T(2,128)S(1)} %get-tuple-element.216, ...), channel_id=1, replica_groups=mesh['band'=64,'lev'=8] {'band','lev'}, use_global_device_ids=true, to_apply=%region_24.25 | all-reduce | flops 6664 | bytes 53312 | tf_op jit(solution)/shard_map/psum | solution.py:135
  478.7 161.8 %all-reduce.50.cloned.1.call-done = f32[2,128,128]{2,1,0:T(8,128)} async-done(((f32[2,128,128]{2,1,0:T(8,128)}), f32[2,128,128]{2,1,0:T(8,128)}) %all-reduce.50.cloned.1.call-update) | async-done | bytes 131088 | tf_op jit(solution)/shard_map/psum | solution.py:135
  640.6 1.6 copy.764
  (477 shorter events, 69.7 us)
Async XLA Ops:
  7.2 26.5 %copy-start = (f32[2,128,128]{2,1,0:T(8,128)S(1)}, f32[2,128,128]{2,1,0:T(8,128)}, u32[]{:S(2)}) copy-start(f32[2,128,128]{2,1,0:T(8,128)} %param.24) | copy-start | bytes 393220
  8.6 26.4 %copy-start.73 = (f32[2,4,128]{2,1,0:T(4,128)S(1)}, f32[2,4,128]{2,1,0:T(4,128)}, u32[]{:S(2)}) copy-start(f32[2,4,128]{2,1,0:T(4,128)} %param.26) | copy-start | bytes 12292
  9.5 25.9 %copy-start.100 = (f32[4]{0:T(128)S(1)}, f32[4]{0:T(128)}, u32[]{:S(2)}) copy-start(f32[4]{0:T(128)} %constant.29.clone) | copy-start | bytes 52
  9.5 26.1 %copy-start.82 = (f32[4,1,2,256]{3,2,1,0:T(2,128)S(1)}, f32[4,1,2,256]{3,2,1,0:T(2,128)}, u32[]{:S(2)}) copy-start(f32[4,1,2,256]{3,2,1,0:T(2,128)} %param.17) | copy-start | bytes 24580
  9.5 30.1 %all-to-all-start.1 = ((f32[2,2,256]{1,0,2:T(2,128)}), f32[2,2,256]{1,0,2:T(2,128)S(1)}, u32[]{:S(2)}, u32[]{:S(2)}) async-start(f32[2,2,256]{1,0,2:T(2,128)} %copy.634), calls=%async_computation.1 | async-start | bytes 524288 | tf_op jit(solution)/shard_map/all_to_all | solution.py:103
  27.6 12.0 %copy-start.49 = (f32[1,4,1,2,257]{4,3,1,2,0:T(2,128)}, f32[1,4,1,2,257]{4,3,1,2,0:T(2,128)S(1)}, u32[]{:S(2)}) copy-start(f32[1,4,1,2,257]{4,3,1,2,0:T(2,128)S(1)} %slice_bitcast_fusion.43) | copy-start | bytes 24676
  29.1 34.0 %copy-start.103 = (f32[128]{0:T(128)}, f32[128]{0:T(128)S(1)}, u32[]{:S(2)}) copy-start(f32[128]{0:T(128)S(1)} %get-tuple-element.178) | copy-start | bytes 1540
  29.1 56.4 %copy-start.105 = (f32[128]{0:T(128)}, f32[128]{0:T(128)S(1)}, u32[]{:S(2)}) copy-start(f32[128]{0:T(128)S(1)} %get-tuple-element.179) | copy-start | bytes 1540
  29.9 34.0 %copy-start.111 = (f32[128]{0:T(128)}, f32[128]{0:T(128)S(1)}, u32[]{:S(2)}) copy-start(f32[128]{0:T(128)S(1)} %get-tuple-element.176) | copy-start | bytes 1540
  29.9 56.3 %copy-start.112 = (f32[128]{0:T(128)}, f32[128]{0:T(128)S(1)}, u32[]{:S(2)}) copy-start(f32[128]{0:T(128)S(1)} %get-tuple-element.177) | copy-start | bytes 1540
  30.6 33.8 %copy-start.104 = (f32[4]{0:T(128)}, f32[4]{0:T(128)S(1)}, u32[]{:S(2)}) copy-start(f32[4]{0:T(128)S(1)} %get-tuple-element.174) | copy-start | bytes 52
  30.6 56.1 %copy-start.107 = (f32[4]{0:T(128)}, f32[4]{0:T(128)S(1)}, u32[]{:S(2)}) copy-start(f32[4]{0:T(128)S(1)} %get-tuple-element.175) | copy-start | bytes 52
  30.7 54.7 %copy-start.91 = (f32[1,514]{1,0:T(1,128)}, f32[1,514]{1,0:T(1,128)S(1)}, u32[]{:S(2)}) copy-start(f32[1,514]{1,0:T(1,128)S(1)} %reshape.1571) | copy-start | bytes 6172
  30.8 54.6 %copy-start.93 = (f32[1,514]{1,0:T(1,128)}, f32[1,514]{1,0:T(1,128)S(1)}, u32[]{:S(2)}) copy-start(f32[1,514]{1,0:T(1,128)S(1)} %reshape.1570) | copy-start | bytes 6172
  31.7 53.7 %copy-start.95 = (f32[1,514]{1,0:T(1,128)}, f32[1,514]{1,0:T(1,128)S(1)}, u32[]{:S(2)}) copy-start(f32[1,514]{1,0:T(1,128)S(1)} %reshape.1569) | copy-start | bytes 6172
  31.8 53.6 %copy-start.97 = (f32[1,514]{1,0:T(1,128)}, f32[1,514]{1,0:T(1,128)S(1)}, u32[]{:S(2)}) copy-start(f32[1,514]{1,0:T(1,128)S(1)} %reshape.1568) | copy-start | bytes 6172
  32.7 52.8 %copy-start.43 = (f32[1,20,128]{2,0,1:T(1,128)}, f32[1,20,128]{2,0,1:T(1,128)S(1)}, u32[]{:S(2)}) copy-start(f32[1,20,128]{2,0,1:T(1,128)S(1)} %get-tuple-element.154) | copy-start | bytes 30724
  32.8 6.8 %copy-start.51 = (f32[1,4,1,2,257]{4,3,1,2,0:T(2,128)}, f32[1,4,1,2,257]{4,3,1,2,0:T(2,128)S(1)}, u32[]{:S(2)}) copy-start(f32[1,4,1,2,257]{4,3,1,2,0:T(2,128)S(1)} %get-tuple-element.155) | copy-start | bytes 24676
  32.8 6.8 %copy-start.53 = (f32[1,4,1,2,257]{4,3,1,2,0:T(2,128)}, f32[1,4,1,2,257]{4,3,1,2,0:T(2,128)S(1)}, u32[]{:S(2)}) copy-start(f32[1,4,1,2,257]{4,3,1,2,0:T(2,128)S(1)} %get-tuple-element.156) | copy-start | bytes 24676
  32.8 6.8 %copy-start.55 = (f32[1,4,1,2,257]{4,3,1,2,0:T(2,128)}, f32[1,4,1,2,257]{4,3,1,2,0:T(2,128)S(1)}, u32[]{:S(2)}) copy-start(f32[1,4,1,2,257]{4,3,1,2,0:T(2,128)S(1)} %get-tuple-element.157) | copy-start | bytes 24676
  39.6 21.6 %all-to-all-start = ((f32[4,1,2,256]{0,2,1,3:T(2,128)}), f32[4,1,2,256]{0,2,1,3:T(2,128)S(1)}, u32[]{:S(2)}, u32[]{:S(2)}) async-start(f32[4,1,2,256]{0,2,1,3:T(2,128)} %copy.631), calls=%async_computation | async-start | bytes 524288 | tf_op jit(solution)/shard_map/all_to_all | solution.py:66
  50.0 13.1 %copy-start.87 = (f32[1,516]{1,0:T(1,128)}, f32[1,516]{1,0:T(1,128)S(1)}, u32[]{:S(2)}) copy-start(f32[1,516]{1,0:T(1,128)S(1)} %reshape.1574) | copy-start | bytes 6196
  50.1 13.0 %copy-start.88 = (f32[1,516]{1,0:T(1,128)}, f32[1,516]{1,0:T(1,128)S(1)}, u32[]{:S(2)}) copy-start(f32[1,516]{1,0:T(1,128)S(1)} %reshape.1573) | copy-start | bytes 6196
  50.3 12.8 %copy-start.89 = (f32[1,516]{1,0:T(1,128)}, f32[1,516]{1,0:T(1,128)S(1)}, u32[]{:S(2)}) copy-start(f32[1,516]{1,0:T(1,128)S(1)} %reshape.1576) | copy-start | bytes 6196
  50.4 12.7 %copy-start.90 = (f32[1,516]{1,0:T(1,128)}, f32[1,516]{1,0:T(1,128)S(1)}, u32[]{:S(2)}) copy-start(f32[1,516]{1,0:T(1,128)S(1)} %reshape.1575) | copy-start | bytes 6196
  110.4 5.9 copy-start.101
  116.6 19.5 %copy-start.92 = (f32[1,514]{1,0:T(1,128)S(1)}, f32[1,514]{1,0:T(1,128)}, u32[]{:S(2)}) copy-start(f32[1,514]{1,0:T(1,128)} %copy-done.91) | copy-start | bytes 6172
  116.6 19.5 %copy-start.94 = (f32[1,514]{1,0:T(1,128)S(1)}, f32[1,514]{1,0:T(1,128)}, u32[]{:S(2)}) copy-start(f32[1,514]{1,0:T(1,128)} %copy-done.93) | copy-start | bytes 6172
  116.7 19.5 %copy-start.96 = (f32[1,514]{1,0:T(1,128)S(1)}, f32[1,514]{1,0:T(1,128)}, u32[]{:S(2)}) copy-start(f32[1,514]{1,0:T(1,128)} %copy-done.95) | copy-start | bytes 6172
  116.7 19.5 %copy-start.98 = (f32[1,514]{1,0:T(1,128)S(1)}, f32[1,514]{1,0:T(1,128)}, u32[]{:S(2)}) copy-start(f32[1,514]{1,0:T(1,128)} %copy-done.97) | copy-start | bytes 6172
  116.7 19.5 %copy-start.44 = (f32[1,20,128]{2,0,1:T(1,128)S(1)}, f32[1,20,128]{2,0,1:T(1,128)}, u32[]{:S(2)}) copy-start(f32[1,20,128]{2,0,1:T(1,128)} %copy-done.43) | copy-start | bytes 30724
  116.7 19.5 %copy-start.106 = (f32[128]{0:T(128)S(1)}, f32[128]{0:T(128)}, u32[]{:S(2)}) copy-start(f32[128]{0:T(128)} %copy-done.105) | copy-start | bytes 1540
  117.1 19.8 %copy-start.113 = (f32[128]{0:T(128)S(1)}, f32[128]{0:T(128)}, u32[]{:S(2)}) copy-start(f32[128]{0:T(128)} %copy-done.112) | copy-start | bytes 1540
  236.9 5.3 copy-start.25
  249.8 5.8 copy-start.13
  249.9 18.6 %copy-start.66 = (f32[1,4,1,2,257]{4,3,1,2,0:T(2,128)S(1)}, f32[1,4,1,2,257]{4,3,1,2,0:T(2,128)}, u32[]{:S(2)}) copy-start(f32[1,4,1,2,257]{4,3,1,2,0:T(2,128)} %copy-done.65) | copy-start | bytes 24676
  249.9 18.6 %copy-start.68 = (f32[1,4,1,2,257]{4,3,1,2,0:T(2,128)S(1)}, f32[1,4,1,2,257]{4,3,1,2,0:T(2,128)}, u32[]{:S(2)}) copy-start(f32[1,4,1,2,257]{4,3,1,2,0:T(2,128)} %copy-done.67) | copy-start | bytes 24676
  249.9 18.6 %copy-start.70 = (f32[1,4,1,2,257]{4,3,1,2,0:T(2,128)S(1)}, f32[1,4,1,2,257]{4,3,1,2,0:T(2,128)}, u32[]{:S(2)}) copy-start(f32[1,4,1,2,257]{4,3,1,2,0:T(2,128)} %copy-done.69) | copy-start | bytes 24676
  250.0 18.6 %copy-start.72 = (f32[1,4,1,2,257]{4,3,1,2,0:T(2,128)S(1)}, f32[1,4,1,2,257]{4,3,1,2,0:T(2,128)}, u32[]{:S(2)}) copy-start(f32[1,4,1,2,257]{4,3,1,2,0:T(2,128)} %copy-done.71) | copy-start | bytes 24676
  250.0 19.6 %copy-start.10 = (f32[514,128]{1,0:T(8,128)S(1)}, f32[514,128]{1,0:T(8,128)}, u32[]{:S(2)}) copy-start(f32[514,128]{1,0:T(8,128)} %copy-done.9) | copy-start | bytes 789508
  250.0 19.6 %copy-start.76 = (f32[2,4,128]{2,1,0:T(4,128)S(1)}, f32[2,4,128]{2,1,0:T(4,128)}, u32[]{:S(2)}) copy-start(f32[2,4,128]{2,1,0:T(4,128)} %param.26) | copy-start | bytes 12292
  250.9 19.9 %copy-start.23 = (f32[514,128]{1,0:T(8,128)S(1)}, f32[514,128]{1,0:T(8,128)}, u32[]{:S(2)}) copy-start(f32[514,128]{1,0:T(8,128)} %copy-done.22) | copy-start | bytes 789508
  250.9 17.3 %all-to-all-start.8 = ((f32[4,1,128,4]{3,0,1,2:T(4,128)}), f32[4,1,128,4]{3,0,1,2:T(4,128)S(1)}, u32[]{:S(2)}, u32[]{:S(2)}) async-start(f32[4,1,128,4]{3,0,1,2:T(4,128)} %copy.671), calls=%async_computation.8 | async-start | bytes 524288 | tf_op jit(solution)/shard_map/all_to_all | solution.py:70
  268.4 4.8 copy-start.41
  275.7 17.6 %all-to-all-start.9 = ((f32[4,1,2,256]{0,2,1,3:T(2,128)}), f32[4,1,2,256]{0,2,1,3:T(2,128)S(1)}, u32[]{:S(2)}, u32[]{:S(2)}) async-start(f32[4,1,2,256]{0,2,1,3:T(2,128)} %copy.677), calls=%async_computation.9 | async-start | bytes 524288 | tf_op jit(solution)/shard_map/all_to_all | solution.py:66
  304.3 5.8 copy-start.86
  304.3 5.8 copy-start.102
  304.4 18.6 %copy-start.58 = (f32[1,4,1,2,257]{4,3,1,2,0:T(2,128)S(1)}, f32[1,4,1,2,257]{4,3,1,2,0:T(2,128)}, u32[]{:S(2)}) copy-start(f32[1,4,1,2,257]{4,3,1,2,0:T(2,128)} %copy-done.57) | copy-start | bytes 24676
  304.4 18.6 %copy-start.60 = (f32[1,4,1,2,257]{4,3,1,2,0:T(2,128)S(1)}, f32[1,4,1,2,257]{4,3,1,2,0:T(2,128)}, u32[]{:S(2)}) copy-start(f32[1,4,1,2,257]{4,3,1,2,0:T(2,128)} %copy-done.59) | copy-start | bytes 24676
  304.4 18.6 %copy-start.62 = (f32[1,4,1,2,257]{4,3,1,2,0:T(2,128)S(1)}, f32[1,4,1,2,257]{4,3,1,2,0:T(2,128)}, u32[]{:S(2)}) copy-start(f32[1,4,1,2,257]{4,3,1,2,0:T(2,128)} %copy-done.61) | copy-start | bytes 24676
  304.5 18.6 %copy-start.64 = (f32[1,4,1,2,257]{4,3,1,2,0:T(2,128)S(1)}, f32[1,4,1,2,257]{4,3,1,2,0:T(2,128)}, u32[]{:S(2)}) copy-start(f32[1,4,1,2,257]{4,3,1,2,0:T(2,128)} %copy-done.63) | copy-start | bytes 24676
  304.5 19.0 %copy-start.6 = (f32[514,128]{1,0:T(8,128)S(1)}, f32[514,128]{1,0:T(8,128)}, u32[]{:S(2)}) copy-start(f32[514,128]{1,0:T(8,128)} %copy-done.5) | copy-start | bytes 789508
  304.5 19.0 %copy-start.77 = (f32[2,4,128]{2,1,0:T(4,128)S(1)}, f32[2,4,128]{2,1,0:T(4,128)}, u32[]{:S(2)}) copy-start(f32[2,4,128]{2,1,0:T(4,128)} %param.26) | copy-start | bytes 12292
  305.3 18.8 %copy-start.19 = (f32[514,128]{1,0:T(8,128)S(1)}, f32[514,128]{1,0:T(8,128)}, u32[]{:S(2)}) copy-start(f32[514,128]{1,0:T(8,128)} %copy-done.18) | copy-start | bytes 789508
  305.4 17.3 %all-to-all-start.10 = ((f32[4,1,128,4]{3,0,1,2:T(4,128)}), f32[4,1,128,4]{3,0,1,2:T(4,128)S(1)}, u32[]{:S(2)}, u32[]{:S(2)}) async-start(f32[4,1,128,4]{3,0,1,2:T(4,128)} %copy.684), calls=%async_computation.10 | async-start | bytes 524288 | tf_op jit(solution)/shard_map/all_to_all | solution.py:70
  327.3 17.3 %all-to-all-start.11 = ((f32[4,1,2,256]{0,2,1,3:T(2,128)}), f32[4,1,2,256]{0,2,1,3:T(2,128)S(1)}, u32[]{:S(2)}, u32[]{:S(2)}) async-start(f32[4,1,2,256]{0,2,1,3:T(2,128)} %copy.690), calls=%async_computation.11 | async-start | bytes 524288 | tf_op jit(solution)/shard_map/all_to_all | solution.py:66
  350.7 18.5 %copy-start.50 = (f32[1,4,1,2,257]{4,3,1,2,0:T(2,128)S(1)}, f32[1,4,1,2,257]{4,3,1,2,0:T(2,128)}, u32[]{:S(2)}) copy-start(f32[1,4,1,2,257]{4,3,1,2,0:T(2,128)} %copy-done.49) | copy-start | bytes 24676
  350.7 18.5 %copy-start.52 = (f32[1,4,1,2,257]{4,3,1,2,0:T(2,128)S(1)}, f32[1,4,1,2,257]{4,3,1,2,0:T(2,128)}, u32[]{:S(2)}) copy-start(f32[1,4,1,2,257]{4,3,1,2,0:T(2,128)} %copy-done.51) | copy-start | bytes 24676
  350.7 18.5 %copy-start.54 = (f32[1,4,1,2,257]{4,3,1,2,0:T(2,128)S(1)}, f32[1,4,1,2,257]{4,3,1,2,0:T(2,128)}, u32[]{:S(2)}) copy-start(f32[1,4,1,2,257]{4,3,1,2,0:T(2,128)} %copy-done.53) | copy-start | bytes 24676
  350.8 18.5 %copy-start.56 = (f32[1,4,1,2,257]{4,3,1,2,0:T(2,128)S(1)}, f32[1,4,1,2,257]{4,3,1,2,0:T(2,128)}, u32[]{:S(2)}) copy-start(f32[1,4,1,2,257]{4,3,1,2,0:T(2,128)} %copy-done.55) | copy-start | bytes 24676
  350.8 19.0 %copy-start.2 = (f32[514,128]{1,0:T(8,128)S(1)}, f32[514,128]{1,0:T(8,128)}, u32[]{:S(2)}) copy-start(f32[514,128]{1,0:T(8,128)} %copy-done.1) | copy-start | bytes 789508
  351.7 18.8 %copy-start.15 = (f32[514,128]{1,0:T(8,128)S(1)}, f32[514,128]{1,0:T(8,128)}, u32[]{:S(2)}) copy-start(f32[514,128]{1,0:T(8,128)} %copy-done.14) | copy-start | bytes 789508
  351.7 17.3 %all-to-all-start.12 = ((f32[4,1,128,4]{3,0,1,2:T(4,128)}), f32[4,1,128,4]{3,0,1,2:T(4,128)S(1)}, u32[]{:S(2)}, u32[]{:S(2)}) async-start(f32[4,1,128,4]{3,0,1,2:T(4,128)} %copy.697), calls=%async_computation.12 | async-start | bytes 524288 | tf_op jit(solution)/shard_map/all_to_all | solution.py:70
  356.4 284.2 %all-reduce.50.cloned.1.call-start = ((), (), s32[]{:S(2)}) async-start(), calls=%async_computation.13 | async-start | bytes 262144 | tf_op jit(solution)/shard_map/psum | solution.py:135
  (67 other events, 141.9 us)
Sparse Core Ops, SparseCore 0:
  373.0 267.4 all-reduce.49
where the time goes:
time: 660 us; the launch traced here: 649 us
  waiting for transfers between devices  235 us (36%)
  blocking collectives  215 us (33%)
  local copies, waits for them, and re-layouts  70 us (11%)
  starting transfers between devices  50.5 us (8%)
  matrix products  39.1 us (6%)
  other arithmetic  22.5 us (3%)
  between operations  16.6 us (3%)
    psum x1, waiting for transfers between devices, on_device(): lax.psum((sums[0], sums[1], sums[2], sums[3], sums[4], sums[5]), ('band',...  162 us
    psum x1, blocking collectives, on_device(): lax.psum((sums[0], sums[1], sums[2], sums[3], sums[4], sums[5]), ('band',...  105 us
    all_to_all x3, blocking collectives, to_rows(): lax.all_to_all(field, 'band', split_axis=2, concat_axis=3, tiled=True)  55.7 us
    all_to_all x3, blocking collectives, to_columns(): lax.all_to_all(field, 'band', split_axis=3, concat_axis=2, tiled=True)  54.9 us
    all_to_all x3, waiting for transfers between devices, to_rows(): lax.all_to_all(field, 'band', split_axis=2, concat_axis=3, tiled=True)  35.5 us
    all_to_all x3, waiting for transfers between devices, to_columns(): lax.all_to_all(field, 'band', split_axis=3, concat_axis=2, tiled=True)  34.8 us
    all_to_all x3, starting transfers between devices, to_columns(): lax.all_to_all(field, 'band', split_axis=3, concat_axis=2, tiled=True)  18.9 us
    all_to_all x1, starting transfers between devices, on_device(): lax.all_to_all(stacked, 'band', split_axis=2, concat_axis=1, tiled=True)  17.3 us
  transfers between devices with their start and end apart: 8, of which 8 were waited for; matrix products, arithmetic and copies ran while one was open for 2% of the time, Pallas kernels for 0%

commit v1 on v0

--- a/solution.py
+++ b/solution.py
@@ -132,7 +132,7 @@
             )
         )
         sums = tuple((earlier + latest for earlier, latest in zip(sums, step_grads)))
-    sums = lax.psum((sums[0], sums[1], sums[2], sums[3], sums[4], sums[5]), ("band", "lev"))
+    sums = lax.psum(lax.psum((sums[0], sums[1], sums[2], sums[3], sums[4], sums[5]), "band"), "lev")
     return (field, sums[0], sums[1], sums[2], sums[3], sums[4], sums[5])
 
 

time: 660 us -> 845 us (1.28)
  blocking collectives: 215 us -> 413 us
  waiting for transfers between devices: 235 us -> 223 us
    psum x1 -> x2, blocking collectives: 105 us -> 303 us  [the longest x1 222 us: on_device(): lax.psum((sums[0], sums[1], sums[2], sums[3], sums[4], sums[5]), 'band')]
    psum x1 -> x2, waiting for transfers between devices: 162 us -> 149 us  [the longest x1 149 us: on_device(): lax.psum((sums[0], sums[1], sums[2], sums[3], sums[4], sums[5]), 'band')]
  transfers between devices with their start and end apart: 8 -> 9, of which waited for: 8 -> 8; matrix products, arithmetic and copies ran while one was open for 2% -> 2% of each run, Pallas kernels for 0% -> 0%
where the time goes in v1:
time: 845 us; the launch traced here: 834 us
  blocking collectives  413 us (49%)
  waiting for transfers between devices  223 us (26%)
  local copies, waits for them, and re-layouts  69.3 us (8%)
  starting transfers between devices  49.8 us (6%)
  matrix products  39.2 us (5%)
  other arithmetic  22.5 us (3%)
  between operations  16.6 us (2%)
    psum x1, blocking collectives, on_device(): lax.psum((sums[0], sums[1], sums[2], sums[3], sums[4], sums[5]), 'band')  222 us
    psum x1, waiting for transfers between devices, on_device(): lax.psum((sums[0], sums[1], sums[2], sums[3], sums[4], sums[5]), 'band')  149 us
    psum x1, blocking collectives, on_device(): lax.psum(lax.psum((sums[0], sums[1], sums[2], sums[3], sums[4], sums[5]),...  80.7 us
    all_to_all x3, blocking collectives, to_rows(): lax.all_to_all(field, 'band', split_axis=2, concat_axis=3, tiled=True)  55.7 us
    all_to_all x3, blocking collectives, to_columns(): lax.all_to_all(field, 'band', split_axis=3, concat_axis=2, tiled=True)  54.9 us
    all_to_all x3, waiting for transfers between devices, to_rows(): lax.all_to_all(field, 'band', split_axis=2, concat_axis=3, tiled=True)  35.5 us
    all_to_all x3, waiting for transfers between devices, to_columns(): lax.all_to_all(field, 'band', split_axis=3, concat_axis=2, tiled=True)  34.8 us
    all_to_all x3, starting transfers between devices, to_columns(): lax.all_to_all(field, 'band', split_axis=3, concat_axis=2, tiled=True)  18.2 us
  transfers between devices with their start and end apart: 9, of which 8 were waited for; matrix products, arithmetic and copies ran while one was open for 2% of the time, Pallas kernels for 0%

profile of v1, /device:TPU:1, one launch (start us, length us, event | category | flops | bytes accessed | tf_op | source)
XLA Modules:
  0.0 833.8 jit_solution(6127829722203833983)
XLA Ops:
  9.5 17.3 %all-to-all-start.1 = ((f32[2,2,256]{1,0,2:T(2,128)}), f32[2,2,256]{1,0,2:T(2,128)S(1)}, u32[]{:S(2)}, u32[]{:S(2)}) async-start(f32[2,2,256]{1,0,2:T(2,128)} %copy.634), calls=%async_computation.1 | async-start | bytes 524288 | tf_op jit(solution)/shard_map/all_to_all | solution.py:103
  35.8 3.7 all-to-all-done.1
  39.6 8.4 %all-to-all-start = ((f32[4,1,2,256]{0,2,1,3:T(2,128)}), f32[4,1,2,256]{0,2,1,3:T(2,128)S(1)}, u32[]{:S(2)}, u32[]{:S(2)}) async-start(f32[4,1,2,256]{0,2,1,3:T(2,128)} %copy.631), calls=%async_computation | async-start | bytes 524288 | tf_op jit(solution)/shard_map/all_to_all | solution.py:66
  49.7 10.8 %all-to-all-done = f32[4,1,2,256]{0,2,1,3:T(2,128)S(1)} async-done(((f32[4,1,2,256]{0,2,1,3:T(2,128)}), f32[4,1,2,256]{0,2,1,3:T(2,128)S(1)}, u32[]{:S(2)}, u32[]{:S(2)}) %all-to-all-start) | async-done | bytes 8224 | tf_op jit(solution)/shard_map/all_to_all | solution.py:66
  65.7 18.4 %all_to_all.231 = f32[4,1,128,4]{3,0,1,2:T(4,128)S(1)} all-to-all(f32[4,1,128,4]{3,0,1,2:T(4,128)S(1)} %copy.642), channel_id=1, replica_groups=mesh['band'=64,'lev'=8] {'band'}, dimensions={2} | all-to-all | bytes 16384 | tf_op jit(solution)/shard_map/all_to_all | solution.py:70
  88.2 18.4 %all_to_all.232 = f32[4,1,2,256]{0,2,1,3:T(2,128)S(1)} all-to-all(f32[4,1,2,256]{0,2,1,3:T(2,128)S(1)} %copy.646), channel_id=1, replica_groups=mesh['band'=64,'lev'=8] {'band'}, dimensions={3} | all-to-all | bytes 16384 | tf_op jit(solution)/shard_map/all_to_all | solution.py:66
  109.6 1.5 concatenate.121
  111.2 1.3 fusion.8
  112.5 1.2 fusion.2
  114.5 1.0 fusion.101
  116.6 18.4 %all_to_all.233 = f32[4,1,128,4]{3,0,1,2:T(4,128)S(1)} all-to-all(f32[4,1,128,4]{3,0,1,2:T(4,128)S(1)} %copy.651), channel_id=1, replica_groups=mesh['band'=64,'lev'=8] {'band'}, dimensions={2} | all-to-all | bytes 16384 | tf_op jit(solution)/shard_map/all_to_all | solution.py:70
  138.9 18.4 %all_to_all.234 = f32[4,1,2,256]{0,2,1,3:T(2,128)S(1)} all-to-all(f32[4,1,2,256]{0,2,1,3:T(2,128)S(1)} %copy.655), channel_id=1, replica_groups=mesh['band'=64,'lev'=8] {'band'}, dimensions={3} | all-to-all | bytes 16384 | tf_op jit(solution)/shard_map/all_to_all | solution.py:66
  160.0 1.5 slice_bitcast_fusion.15
  161.5 1.1 pad_maximum_fusion.2
  162.6 2.2 reshape.1580
  164.8 2.7 concatenate.123
  167.5 1.5 fusion.6
  169.0 1.2 fusion
  170.9 1.0 fusion.103
  172.0 1.3 add_bitcast_fusion
  173.3 1.6 mul.546
  174.9 1.9 multiply_reduce_fusion
  176.7 1.7 copy.716
  179.2 1.4 fusion.44
  180.6 1.6 copy.660
  182.1 18.8 %all_to_all.235 = f32[4,1,128,4]{3,0,1,2:T(4,128)S(1)} all-to-all(f32[4,1,128,4]{3,0,1,2:T(4,128)} %copy.660), channel_id=1, replica_groups=mesh['band'=64,'lev'=8] {'band'}, dimensions={2} | all-to-all | bytes 16384 | tf_op jit(solution)/shard_map/all_to_all | solution.py:70
  201.8 1.7 all_to_all.193
  203.5 1.3 fusion.50
  204.8 1.6 copy.664
  206.3 18.1 %all_to_all.236 = f32[4,1,2,256]{0,2,1,3:T(2,128)} all-to-all(f32[4,1,2,256]{0,2,1,3:T(2,128)} %copy.664), channel_id=1, replica_groups=mesh['band'=64,'lev'=8] {'band'}, dimensions={3} | all-to-all | bytes 16384 | tf_op jit(solution)/shard_map/all_to_all | solution.py:66
  224.5 2.7 copy.711
  227.1 1.9 copy.666
  229.0 1.7 copy.667
  231.4 1.4 multiply_bitcast_fusion.2
  232.7 1.6 copy.669
  234.3 1.9 multiply_reduce_fusion.7
  236.9 1.7 reshape.1587
  238.6 1.6 fusion.90
  240.4 1.2 fusion.110
  241.6 1.3 convolution_bitcast_fusion.4
  242.9 1.1 fusion.104
  245.9 1.1 reshape.1581
  247.0 1.1 bitcast_add_fusion.2
  250.2 4.8 all-to-all-start.8
  255.0 1.5 convolution_bitcast_fusion.21
  256.5 11.0 %all-to-all-done.8 = f32[4,1,128,4]{3,0,1,2:T(4,128)S(1)} async-done(((f32[4,1,128,4]{3,0,1,2:T(4,128)}), f32[4,1,128,4]{3,0,1,2:T(4,128)S(1)}, u32[]{:S(2)}, u32[]{:S(2)}) %all-to-all-start.8) | async-done | bytes 8224 | tf_op jit(solution)/shard_map/all_to_all | solution.py:70
  268.9 1.2 fusion.111
  270.1 1.3 convolution_bitcast_fusion.5
  271.4 1.2 fusion.105
  275.0 5.0 all-to-all-start.9
  280.9 11.8 %all-to-all-done.9 = f32[4,1,2,256]{0,2,1,3:T(2,128)S(1)} async-done(((f32[4,1,2,256]{0,2,1,3:T(2,128)}), f32[4,1,2,256]{0,2,1,3:T(2,128)S(1)}, u32[]{:S(2)}, u32[]{:S(2)}) %all-to-all-start.9) | async-done | bytes 8224 | tf_op jit(solution)/shard_map/all_to_all | solution.py:66
  297.3 1.2 fusion.112
  298.5 1.3 convolution_bitcast_fusion.2
  299.9 1.1 fusion.106
  304.7 4.7 all-to-all-start.10
  309.7 12.3 %all-to-all-done.10 = f32[4,1,128,4]{3,0,1,2:T(4,128)S(1)} async-done(((f32[4,1,128,4]{3,0,1,2:T(4,128)}), f32[4,1,128,4]{3,0,1,2:T(4,128)S(1)}, u32[]{:S(2)}, u32[]{:S(2)}) %all-to-all-start.10) | async-done | bytes 8224 | tf_op jit(solution)/shard_map/all_to_all | solution.py:70
  326.6 4.8 all-to-all-start.11
  331.6 12.3 %all-to-all-done.11 = f32[4,1,2,256]{0,2,1,3:T(2,128)S(1)} async-done(((f32[4,1,2,256]{0,2,1,3:T(2,128)}), f32[4,1,2,256]{0,2,1,3:T(2,128)S(1)}, u32[]{:S(2)}, u32[]{:S(2)}) %all-to-all-start.11) | async-done | bytes 8224 | tf_op jit(solution)/shard_map/all_to_all | solution.py:66
  351.0 4.8 all-to-all-start.12
  356.1 12.2 %all-to-all-done.12 = f32[4,1,128,4]{3,0,1,2:T(4,128)S(1)} async-done(((f32[4,1,128,4]{3,0,1,2:T(4,128)}), f32[4,1,128,4]{3,0,1,2:T(4,128)S(1)}, u32[]{:S(2)}, u32[]{:S(2)}) %all-to-all-start.12) | async-done | bytes 8224 | tf_op jit(solution)/shard_map/all_to_all | solution.py:70
  372.7 149.0 %all-reduce.52.cloned.1.call-done = f32[2,128,128]{2,1,0:T(8,128)} async-done(((f32[2,128,128]{2,1,0:T(8,128)}), f32[2,128,128]{2,1,0:T(8,128)}) %all-reduce.52.cloned.1.call-update) | async-done | bytes 131088 | tf_op jit(solution)/shard_map/psum | solution.py:135
  521.8 222.1 %all-reduce.47 = (f32[2,20,128]{2,1,0:T(8,128)S(1)}, f32[2,128]{1,0:T(2,128)S(1)}, f32[2,128]{1,0:T(2,128)S(1)}, f32[2,4,128]{2,1,0:T(4,128)S(1)}, f32[2,4]{1,0:T(2,128)S(1)}) all-reduce(f32[2,20,128]{2,1,0:T(8,128)S(1)} %fusion.37, f32[2,128]{1,0:T(2,128)S(1)} %get-tuple-element.221, ...), channel_id=1, replica_groups=mesh['band'=64,'lev'=8] {'band'}, use_global_device_ids=true, to_apply=%region_24.25 | all-reduce | flops 6664 | bytes 53312 | tf_op jit(solution)/shard_map/psum | solution.py:135
  743.9 80.7 %all-reduce.48 = (f32[2,20,128]{2,1,0:T(8,128)S(1)}, f32[2,128]{1,0:T(2,128)}, f32[2,128]{1,0:T(2,128)}, f32[2,4,128]{2,1,0:T(4,128)}, f32[2,4]{1,0:T(2,128)}) all-reduce(f32[2,20,128]{2,1,0:T(8,128)S(1)} %get-tuple-element.96, f32[2,128]{1,0:T(2,128)S(1)} %get-tuple-element.97, ...), channel_id=1, replica_groups=mesh['band'=64,'lev'=8] {'lev'}, use_global_device_ids=true, to_apply=%region_25.26 | all-reduce | flops 6664 | bytes 53312 | tf_op jit(solution)/shard_map/psum | solution.py:135
  825.2 1.6 copy.765
  (481 shorter events, 70.0 us)
Async XLA Ops:
  7.2 26.5 %copy-start = (f32[2,128,128]{2,1,0:T(8,128)S(1)}, f32[2,128,128]{2,1,0:T(8,128)}, u32[]{:S(2)}) copy-start(f32[2,128,128]{2,1,0:T(8,128)} %param.24) | copy-start | bytes 393220
  8.6 25.7 %copy-start.73 = (f32[2,4,128]{2,1,0:T(4,128)S(1)}, f32[2,4,128]{2,1,0:T(4,128)}, u32[]{:S(2)}) copy-start(f32[2,4,128]{2,1,0:T(4,128)} %param.26) | copy-start | bytes 12292
  9.5 25.2 %copy-start.100 = (f32[4]{0:T(128)S(1)}, f32[4]{0:T(128)}, u32[]{:S(2)}) copy-start(f32[4]{0:T(128)} %constant.29.clone) | copy-start | bytes 52
  9.5 25.4 %copy-start.82 = (f32[4,1,2,256]{3,2,1,0:T(2,128)S(1)}, f32[4,1,2,256]{3,2,1,0:T(2,128)}, u32[]{:S(2)}) copy-start(f32[4,1,2,256]{3,2,1,0:T(2,128)} %param.17) | copy-start | bytes 24580
  9.5 30.1 %all-to-all-start.1 = ((f32[2,2,256]{1,0,2:T(2,128)}), f32[2,2,256]{1,0,2:T(2,128)S(1)}, u32[]{:S(2)}, u32[]{:S(2)}) async-start(f32[2,2,256]{1,0,2:T(2,128)} %copy.634), calls=%async_computation.1 | async-start | bytes 524288 | tf_op jit(solution)/shard_map/all_to_all | solution.py:103
  27.6 12.0 %copy-start.49 = (f32[1,4,1,2,257]{4,3,1,2,0:T(2,128)}, f32[1,4,1,2,257]{4,3,1,2,0:T(2,128)S(1)}, u32[]{:S(2)}) copy-start(f32[1,4,1,2,257]{4,3,1,2,0:T(2,128)S(1)} %slice_bitcast_fusion.43) | copy-start | bytes 24676
  29.1 33.3 %copy-start.103 = (f32[128]{0:T(128)}, f32[128]{0:T(128)S(1)}, u32[]{:S(2)}) copy-start(f32[128]{0:T(128)S(1)} %get-tuple-element.183) | copy-start | bytes 1540
  29.1 55.6 %copy-start.105 = (f32[128]{0:T(128)}, f32[128]{0:T(128)S(1)}, u32[]{:S(2)}) copy-start(f32[128]{0:T(128)S(1)} %get-tuple-element.184) | copy-start | bytes 1540
  29.9 33.2 %copy-start.111 = (f32[128]{0:T(128)}, f32[128]{0:T(128)S(1)}, u32[]{:S(2)}) copy-start(f32[128]{0:T(128)S(1)} %get-tuple-element.181) | copy-start | bytes 1540
  29.9 55.6 %copy-start.112 = (f32[128]{0:T(128)}, f32[128]{0:T(128)S(1)}, u32[]{:S(2)}) copy-start(f32[128]{0:T(128)S(1)} %get-tuple-element.182) | copy-start | bytes 1540
  30.6 33.1 %copy-start.104 = (f32[4]{0:T(128)}, f32[4]{0:T(128)S(1)}, u32[]{:S(2)}) copy-start(f32[4]{0:T(128)S(1)} %get-tuple-element.179) | copy-start | bytes 52
  30.6 55.4 %copy-start.107 = (f32[4]{0:T(128)}, f32[4]{0:T(128)S(1)}, u32[]{:S(2)}) copy-start(f32[4]{0:T(128)S(1)} %get-tuple-element.180) | copy-start | bytes 52
  30.7 54.0 %copy-start.91 = (f32[1,514]{1,0:T(1,128)}, f32[1,514]{1,0:T(1,128)S(1)}, u32[]{:S(2)}) copy-start(f32[1,514]{1,0:T(1,128)S(1)} %reshape.1571) | copy-start | bytes 6172
  30.8 53.9 %copy-start.93 = (f32[1,514]{1,0:T(1,128)}, f32[1,514]{1,0:T(1,128)S(1)}, u32[]{:S(2)}) copy-start(f32[1,514]{1,0:T(1,128)S(1)} %reshape.1570) | copy-start | bytes 6172
  31.7 53.0 %copy-start.95 = (f32[1,514]{1,0:T(1,128)}, f32[1,514]{1,0:T(1,128)S(1)}, u32[]{:S(2)}) copy-start(f32[1,514]{1,0:T(1,128)S(1)} %reshape.1569) | copy-start | bytes 6172
  31.8 52.9 %copy-start.97 = (f32[1,514]{1,0:T(1,128)}, f32[1,514]{1,0:T(1,128)S(1)}, u32[]{:S(2)}) copy-start(f32[1,514]{1,0:T(1,128)S(1)} %reshape.1568) | copy-start | bytes 6172
  32.6 52.1 %copy-start.43 = (f32[1,20,128]{2,0,1:T(1,128)}, f32[1,20,128]{2,0,1:T(1,128)S(1)}, u32[]{:S(2)}) copy-start(f32[1,20,128]{2,0,1:T(1,128)S(1)} %get-tuple-element.159) | copy-start | bytes 30724
  32.7 6.8 copy-start.51
  32.8 6.8 copy-start.53
  32.8 6.8 copy-start.55
  33.6 15.3 %copy-start.14 = (f32[514,128]{1,0:T(8,128)}, f32[514,128]{1,0:T(8,128)S(1)}, u32[]{:S(2)}) copy-start(f32[514,128]{1,0:T(8,128)S(1)} %fusion.11) | copy-start | bytes 789508
  34.2 14.9 %copy-start.1 = (f32[514,128]{1,0:T(8,128)}, f32[514,128]{1,0:T(8,128)S(1)}, u32[]{:S(2)}) copy-start(f32[514,128]{1,0:T(8,128)S(1)} %fusion.5) | copy-start | bytes 789508
  39.6 20.9 %all-to-all-start = ((f32[4,1,2,256]{0,2,1,3:T(2,128)}), f32[4,1,2,256]{0,2,1,3:T(2,128)S(1)}, u32[]{:S(2)}, u32[]{:S(2)}) async-start(f32[4,1,2,256]{0,2,1,3:T(2,128)} %copy.631), calls=%async_computation | async-start | bytes 524288 | tf_op jit(solution)/shard_map/all_to_all | solution.py:66
  49.2 13.1 %copy-start.87 = (f32[1,516]{1,0:T(1,128)}, f32[1,516]{1,0:T(1,128)S(1)}, u32[]{:S(2)}) copy-start(f32[1,516]{1,0:T(1,128)S(1)} %reshape.1574) | copy-start | bytes 6196
  49.4 13.0 %copy-start.88 = (f32[1,516]{1,0:T(1,128)}, f32[1,516]{1,0:T(1,128)S(1)}, u32[]{:S(2)}) copy-start(f32[1,516]{1,0:T(1,128)S(1)} %reshape.1573) | copy-start | bytes 6196
  49.6 12.8 %copy-start.89 = (f32[1,516]{1,0:T(1,128)}, f32[1,516]{1,0:T(1,128)S(1)}, u32[]{:S(2)}) copy-start(f32[1,516]{1,0:T(1,128)S(1)} %reshape.1576) | copy-start | bytes 6196
  49.7 12.7 %copy-start.90 = (f32[1,516]{1,0:T(1,128)}, f32[1,516]{1,0:T(1,128)S(1)}, u32[]{:S(2)}) copy-start(f32[1,516]{1,0:T(1,128)S(1)} %reshape.1575) | copy-start | bytes 6196
  115.9 19.5 %copy-start.92 = (f32[1,514]{1,0:T(1,128)S(1)}, f32[1,514]{1,0:T(1,128)}, u32[]{:S(2)}) copy-start(f32[1,514]{1,0:T(1,128)} %copy-done.91) | copy-start | bytes 6172
  115.9 19.5 %copy-start.94 = (f32[1,514]{1,0:T(1,128)S(1)}, f32[1,514]{1,0:T(1,128)}, u32[]{:S(2)}) copy-start(f32[1,514]{1,0:T(1,128)} %copy-done.93) | copy-start | bytes 6172
  116.0 19.5 %copy-start.96 = (f32[1,514]{1,0:T(1,128)S(1)}, f32[1,514]{1,0:T(1,128)}, u32[]{:S(2)}) copy-start(f32[1,514]{1,0:T(1,128)} %copy-done.95) | copy-start | bytes 6172
  116.0 19.5 %copy-start.98 = (f32[1,514]{1,0:T(1,128)S(1)}, f32[1,514]{1,0:T(1,128)}, u32[]{:S(2)}) copy-start(f32[1,514]{1,0:T(1,128)} %copy-done.97) | copy-start | bytes 6172
  116.0 19.5 %copy-start.44 = (f32[1,20,128]{2,0,1:T(1,128)S(1)}, f32[1,20,128]{2,0,1:T(1,128)}, u32[]{:S(2)}) copy-start(f32[1,20,128]{2,0,1:T(1,128)} %copy-done.43) | copy-start | bytes 30724
  116.0 19.5 %copy-start.106 = (f32[128]{0:T(128)S(1)}, f32[128]{0:T(128)}, u32[]{:S(2)}) copy-start(f32[128]{0:T(128)} %copy-done.105) | copy-start | bytes 1540
  116.4 19.8 %copy-start.113 = (f32[128]{0:T(128)S(1)}, f32[128]{0:T(128)}, u32[]{:S(2)}) copy-start(f32[128]{0:T(128)} %copy-done.112) | copy-start | bytes 1540
  249.3 18.6 %copy-start.66 = (f32[1,4,1,2,257]{4,3,1,2,0:T(2,128)S(1)}, f32[1,4,1,2,257]{4,3,1,2,0:T(2,128)}, u32[]{:S(2)}) copy-start(f32[1,4,1,2,257]{4,3,1,2,0:T(2,128)} %copy-done.65) | copy-start | bytes 24676
  249.3 18.6 %copy-start.68 = (f32[1,4,1,2,257]{4,3,1,2,0:T(2,128)S(1)}, f32[1,4,1,2,257]{4,3,1,2,0:T(2,128)}, u32[]{:S(2)}) copy-start(f32[1,4,1,2,257]{4,3,1,2,0:T(2,128)} %copy-done.67) | copy-start | bytes 24676
  249.3 18.6 %copy-start.70 = (f32[1,4,1,2,257]{4,3,1,2,0:T(2,128)S(1)}, f32[1,4,1,2,257]{4,3,1,2,0:T(2,128)}, u32[]{:S(2)}) copy-start(f32[1,4,1,2,257]{4,3,1,2,0:T(2,128)} %copy-done.69) | copy-start | bytes 24676
  249.3 18.6 %copy-start.72 = (f32[1,4,1,2,257]{4,3,1,2,0:T(2,128)S(1)}, f32[1,4,1,2,257]{4,3,1,2,0:T(2,128)}, u32[]{:S(2)}) copy-start(f32[1,4,1,2,257]{4,3,1,2,0:T(2,128)} %copy-done.71) | copy-start | bytes 24676
  249.3 19.6 %copy-start.10 = (f32[514,128]{1,0:T(8,128)S(1)}, f32[514,128]{1,0:T(8,128)}, u32[]{:S(2)}) copy-start(f32[514,128]{1,0:T(8,128)} %copy-done.9) | copy-start | bytes 789508
  249.3 19.6 %copy-start.76 = (f32[2,4,128]{2,1,0:T(4,128)S(1)}, f32[2,4,128]{2,1,0:T(4,128)}, u32[]{:S(2)}) copy-start(f32[2,4,128]{2,1,0:T(4,128)} %param.26) | copy-start | bytes 12292
  250.2 19.9 %copy-start.23 = (f32[514,128]{1,0:T(8,128)S(1)}, f32[514,128]{1,0:T(8,128)}, u32[]{:S(2)}) copy-start(f32[514,128]{1,0:T(8,128)} %copy-done.22) | copy-start | bytes 789508
  250.2 17.3 %all-to-all-start.8 = ((f32[4,1,128,4]{3,0,1,2:T(4,128)}), f32[4,1,128,4]{3,0,1,2:T(4,128)S(1)}, u32[]{:S(2)}, u32[]{:S(2)}) async-start(f32[4,1,128,4]{3,0,1,2:T(4,128)} %copy.671), calls=%async_computation.8 | async-start | bytes 524288 | tf_op jit(solution)/shard_map/all_to_all | solution.py:70
  275.0 17.6 %all-to-all-start.9 = ((f32[4,1,2,256]{0,2,1,3:T(2,128)}), f32[4,1,2,256]{0,2,1,3:T(2,128)S(1)}, u32[]{:S(2)}, u32[]{:S(2)}) async-start(f32[4,1,2,256]{0,2,1,3:T(2,128)} %copy.677), calls=%async_computation.9 | async-start | bytes 524288 | tf_op jit(solution)/shard_map/all_to_all | solution.py:66
  303.8 18.6 %copy-start.58 = (f32[1,4,1,2,257]{4,3,1,2,0:T(2,128)S(1)}, f32[1,4,1,2,257]{4,3,1,2,0:T(2,128)}, u32[]{:S(2)}) copy-start(f32[1,4,1,2,257]{4,3,1,2,0:T(2,128)} %copy-done.57) | copy-start | bytes 24676
  303.8 18.6 %copy-start.60 = (f32[1,4,1,2,257]{4,3,1,2,0:T(2,128)S(1)}, f32[1,4,1,2,257]{4,3,1,2,0:T(2,128)}, u32[]{:S(2)}) copy-start(f32[1,4,1,2,257]{4,3,1,2,0:T(2,128)} %copy-done.59) | copy-start | bytes 24676
  303.8 18.6 %copy-start.62 = (f32[1,4,1,2,257]{4,3,1,2,0:T(2,128)S(1)}, f32[1,4,1,2,257]{4,3,1,2,0:T(2,128)}, u32[]{:S(2)}) copy-start(f32[1,4,1,2,257]{4,3,1,2,0:T(2,128)} %copy-done.61) | copy-start | bytes 24676
  303.8 18.6 %copy-start.64 = (f32[1,4,1,2,257]{4,3,1,2,0:T(2,128)S(1)}, f32[1,4,1,2,257]{4,3,1,2,0:T(2,128)}, u32[]{:S(2)}) copy-start(f32[1,4,1,2,257]{4,3,1,2,0:T(2,128)} %copy-done.63) | copy-start | bytes 24676
  303.8 19.0 %copy-start.6 = (f32[514,128]{1,0:T(8,128)S(1)}, f32[514,128]{1,0:T(8,128)}, u32[]{:S(2)}) copy-start(f32[514,128]{1,0:T(8,128)} %copy-done.5) | copy-start | bytes 789508
  303.8 19.0 %copy-start.77 = (f32[2,4,128]{2,1,0:T(4,128)S(1)}, f32[2,4,128]{2,1,0:T(4,128)}, u32[]{:S(2)}) copy-start(f32[2,4,128]{2,1,0:T(4,128)} %param.26) | copy-start | bytes 12292
  304.7 18.8 %copy-start.19 = (f32[514,128]{1,0:T(8,128)S(1)}, f32[514,128]{1,0:T(8,128)}, u32[]{:S(2)}) copy-start(f32[514,128]{1,0:T(8,128)} %copy-done.18) | copy-start | bytes 789508
  304.7 17.3 %all-to-all-start.10 = ((f32[4,1,128,4]{3,0,1,2:T(4,128)}), f32[4,1,128,4]{3,0,1,2:T(4,128)S(1)}, u32[]{:S(2)}, u32[]{:S(2)}) async-start(f32[4,1,128,4]{3,0,1,2:T(4,128)} %copy.684), calls=%async_computation.10 | async-start | bytes 524288 | tf_op jit(solution)/shard_map/all_to_all | solution.py:70
  326.6 17.3 %all-to-all-start.11 = ((f32[4,1,2,256]{0,2,1,3:T(2,128)}), f32[4,1,2,256]{0,2,1,3:T(2,128)S(1)}, u32[]{:S(2)}, u32[]{:S(2)}) async-start(f32[4,1,2,256]{0,2,1,3:T(2,128)} %copy.690), calls=%async_computation.11 | async-start | bytes 524288 | tf_op jit(solution)/shard_map/all_to_all | solution.py:66
  350.1 18.5 %copy-start.50 = (f32[1,4,1,2,257]{4,3,1,2,0:T(2,128)S(1)}, f32[1,4,1,2,257]{4,3,1,2,0:T(2,128)}, u32[]{:S(2)}) copy-start(f32[1,4,1,2,257]{4,3,1,2,0:T(2,128)} %copy-done.49) | copy-start | bytes 24676
  350.1 18.5 %copy-start.52 = (f32[1,4,1,2,257]{4,3,1,2,0:T(2,128)S(1)}, f32[1,4,1,2,257]{4,3,1,2,0:T(2,128)}, u32[]{:S(2)}) copy-start(f32[1,4,1,2,257]{4,3,1,2,0:T(2,128)} %copy-done.51) | copy-start | bytes 24676
  350.1 18.5 %copy-start.54 = (f32[1,4,1,2,257]{4,3,1,2,0:T(2,128)S(1)}, f32[1,4,1,2,257]{4,3,1,2,0:T(2,128)}, u32[]{:S(2)}) copy-start(f32[1,4,1,2,257]{4,3,1,2,0:T(2,128)} %copy-done.53) | copy-start | bytes 24676
  350.1 18.5 %copy-start.56 = (f32[1,4,1,2,257]{4,3,1,2,0:T(2,128)S(1)}, f32[1,4,1,2,257]{4,3,1,2,0:T(2,128)}, u32[]{:S(2)}) copy-start(f32[1,4,1,2,257]{4,3,1,2,0:T(2,128)} %copy-done.55) | copy-start | bytes 24676
  350.1 19.0 %copy-start.2 = (f32[514,128]{1,0:T(8,128)S(1)}, f32[514,128]{1,0:T(8,128)}, u32[]{:S(2)}) copy-start(f32[514,128]{1,0:T(8,128)} %copy-done.1) | copy-start | bytes 789508
  351.0 18.8 %copy-start.15 = (f32[514,128]{1,0:T(8,128)S(1)}, f32[514,128]{1,0:T(8,128)}, u32[]{:S(2)}) copy-start(f32[514,128]{1,0:T(8,128)} %copy-done.14) | copy-start | bytes 789508
  351.0 17.3 %all-to-all-start.12 = ((f32[4,1,128,4]{3,0,1,2:T(4,128)}), f32[4,1,128,4]{3,0,1,2:T(4,128)S(1)}, u32[]{:S(2)}, u32[]{:S(2)}) async-start(f32[4,1,128,4]{3,0,1,2:T(4,128)} %copy.697), calls=%async_computation.12 | async-start | bytes 524288 | tf_op jit(solution)/shard_map/all_to_all | solution.py:70
  355.8 166.0 %all-reduce.52.cloned.1.call-start = ((), (), s32[]{:S(2)}) async-start(), calls=%async_computation.13 | async-start | bytes 262144 | tf_op jit(solution)/shard_map/psum | solution.py:135
  370.6 151.2 %copy-start.120 = (f32[4]{0:T(128)S(1)}, f32[4]{0:T(128)}, u32[]{:S(2)}) copy-start(f32[4]{0:T(128)} %get-tuple-element.114) | copy-start | bytes 52
  370.6 151.2 %copy-start.121 = (f32[4]{0:T(128)S(1)}, f32[4]{0:T(128)}, u32[]{:S(2)}) copy-start(f32[4]{0:T(128)} %get-tuple-element.116) | copy-start | bytes 52
  370.6 151.2 %copy-start.122 = (f32[4]{0:T(128)S(1)}, f32[4]{0:T(128)}, u32[]{:S(2)}) copy-start(f32[4]{0:T(128)} %get-tuple-element.112) | copy-start | bytes 52
  372.3 452.9 %all-reduce.54.cloned.1.call-start = ((), (), s32[]{:S(2)}) async-start(), calls=%async_computation.14 | async-start | bytes 262144 | tf_op jit(solution)/shard_map/psum | solution.py:135
  (68 other events, 167.6 us)
Sparse Core Ops, SparseCore 0:
  372.4 149.3 all-reduce.51
  524.1 70.5 all-reduce.53
